TPU v7x, 512 devices: a whole 4x4x16 slice. The times are simulated.
512 devices in a mesh: lev: 32 (over x_lo, z), mem: 16 (over x_hi, y, core).
Axes of the slice: x: 4 (x_hi: 2, x_lo: 2; x = x_hi * 2 + x_lo), y: 4, z: 16, core: 2. Of those that a mesh axis runs over, the one named last changes fastest.
Arguments:
- control: bfloat16 [32, 5, 128, 4096], P('mem', None, 'lev'), may hold values from -6 to 6
- static_control_vector: bfloat16 [5, 128, 4096], P(None, None, 'lev'), may hold values from -6 to 6
- perturb: bfloat16 [32, 5, 128, 4096], P('mem', None, None, 'lev'), may hold values from -6 to 6
- tiles: bfloat16 [4, 64, 64], replicated, may hold values from -0.375 to 0.375
- block_offset: int32 [64, 4], replicated, may hold values from -8 to 8
- vert: bfloat16 [5, 128, 128], replicated, may hold values from -0.5 to 0.5
- static_vertical_root: bfloat16 [5, 128, 128], replicated, may hold values from -0.5 to 0.5
- obs_index: int32 [524288], P(('lev', 'mem')), may hold values from 0 to 5119
- obs_value: float32 [524288], P(('lev', 'mem')), may hold values from -6 to 6
- obs_sigma: float32 [524288], P(('lev', 'mem')), may hold values from 0.3 to 1
- huber_mask: int32 [524288], P(('lev', 'mem')), may hold values 0 or 1
Outputs:
- control_out: bfloat16 [32, 5, 128, 4096], P('mem', None, 'lev')
- static_out: bfloat16 [5, 128, 4096], P(None, None, 'lev')
Inputs may be any that keep to these rules, and one draw needn't show every extreme that they name: `obs_index`: indices count in the block held by the observation's own device: 5 variables, 128 / 16 levels, 128 columns, in that order. `block_offset`: source blocks wrap around the window.
All inputs are finite; a program needn't handle non-finite values. No bound on the sum of `huber_mask` on one device may be relied on, other than what follows from the above.
Results may differ from a plain program's by a relative error of at most 0.0057.
Values may be sent and summed in bfloat16 or wider, within the bound.
No kernel may reach another device: no remote copies, remote signals or barrier semaphores. Data moves between devices by JAX's collectives and lax.ppermute only.
A program may use at most 64 MiB of HBM per device.

v0:
```python
import math
import jax
import jax.numpy as jnp
from jax import lax
from jax.sharding import PartitionSpec as P

ITERS = 2
ENS_W = 0.85
STATIC_WEIGHT = 0.5
TAU = 0.5
HUBER_LOW = 0.3


def selectors(block_offset):
    count = block_offset.shape[0]
    blocks = jnp.arange(count, dtype=jnp.int32)
    source = (blocks[:, None] + block_offset) % count
    return (source.T[:, :, None] == blocks[None, None, :]).astype(jnp.bfloat16)


def horizontal(field, tiles, picks):
    count = picks.shape[1]
    width = tiles.shape[1]
    shaped = field.reshape(field.shape[:-1] + (count, width))
    total = None
    for slot in range(tiles.shape[0]):
        moved = jnp.einsum(
            "bj,...jc->...bc", picks[slot], shaped, preferred_element_type=jnp.float32
        ).astype(jnp.bfloat16)
        term = jnp.einsum("...bc,cd->...bd", moved, tiles[slot], preferred_element_type=jnp.float32)
        total = term if total is None else total + term
    return total.reshape(field.shape).astype(jnp.bfloat16)


def horizontal_adjoint(field, tiles, picks):
    count = picks.shape[1]
    width = tiles.shape[1]
    shaped = field.reshape(field.shape[:-1] + (count, width))
    total = None
    for slot in range(tiles.shape[0]):
        term = jnp.einsum(
            "...bc,dc->...bd", shaped, tiles[slot], preferred_element_type=jnp.float32
        )
        moved = jnp.einsum(
            "bj,...bd->...jd",
            picks[slot].astype(jnp.float32),
            term,
            precision=lax.Precision.HIGHEST,
        )
        total = moved if total is None else total + moved
    return total.reshape(field.shape)


def observe(block, obs_index, obs_value, precision_obs):
    flat = block.reshape(-1)
    seen = flat[obs_index]
    resid = precision_obs * (seen - obs_value)
    return jnp.zeros_like(flat).at[obs_index].add(resid).reshape(block.shape)


def on_device(
    control,
    static_control_vector,
    perturb,
    tiles,
    block_offset,
    vert,
    static_vertical_root,
    obs_index,
    obs_value,
    obs_sigma,
    huber_mask,
):
    picks = selectors(block_offset)
    members_all = control.shape[0] * lax.axis_size("mem")
    ens_gain = ENS_W / math.sqrt(members_all)
    level_rows = static_control_vector.shape[1] // lax.axis_size("mem")
    first_level = lax.axis_index("mem") * level_rows
    weights = jnp.where(huber_mask == 1, jnp.float32(1.0), jnp.float32(HUBER_LOW))
    precision_obs = weights / (obs_sigma * obs_sigma)
    vertical_forward = vert.astype(jnp.float32)
    static_forward = static_vertical_root.astype(jnp.float32)
    for turn in range(ITERS):
        local = horizontal(control, tiles, picks)
        columns = lax.all_to_all(local, "lev", split_axis=3, concat_axis=2, tiled=True)
        vertical = jnp.einsum("vlk,mvkc->mvlc", vert, columns, preferred_element_type=jnp.float32)
        partial_value = jnp.sum(vertical * perturb.astype(jnp.float32), axis=0)
        static_portion = jnp.einsum(
            "tbu,tuo->tbo",
            static_vertical_root,
            static_control_vector,
            preferred_element_type=jnp.float32,
        )
        ens = lax.psum(partial_value, "mem")
        increment = ens_gain * ens + STATIC_WEIGHT * static_portion
        own_block = lax.dynamic_slice_in_dim(increment, first_level, level_rows, 1)
        grad_block = observe(own_block, obs_index, obs_value, precision_obs)
        placed = lax.dynamic_update_slice_in_dim(
            jnp.zeros_like(increment), grad_block, first_level, 1
        )
        gradient_field_total = lax.psum(placed, "mem")
        static_gradient = static_control_vector.astype(jnp.float32) + STATIC_WEIGHT * jnp.einsum(
            "otn,ote->one", static_forward, gradient_field_total, precision=lax.Precision.HIGHEST
        )
        weighted_innovations = (ens_gain * gradient_field_total)[None] * perturb.astype(jnp.float32)
        backward_field = jnp.einsum(
            "vkl,mvkc->mvlc",
            vertical_forward,
            weighted_innovations,
            precision=lax.Precision.HIGHEST,
        ).astype(jnp.bfloat16)
        levels = lax.all_to_all(backward_field, "lev", split_axis=2, concat_axis=3, tiled=True)
        adjoint = horizontal_adjoint(levels, tiles, picks)
        current = control.astype(jnp.float32)
        control = (current - TAU * (current + adjoint)).astype(jnp.bfloat16)
        static_control_vector = (
            static_control_vector.astype(jnp.float32) - TAU * static_gradient
        ).astype(jnp.bfloat16)
    return (control, static_control_vector)


def solution(mesh):
    placed = (
        P("mem", None, "lev", None),
        P(None, None, "lev"),
        P("mem", None, None, "lev"),
        P(),
        P(),
        P(),
        P(),
        P(("lev", "mem")),
        P(("lev", "mem")),
        P(("lev", "mem")),
        P(("lev", "mem")),
    )
    return jax.shard_map(
        on_device,
        mesh=mesh,
        in_specs=placed,
        out_specs=(P("mem", None, "lev", None), P(None, None, "lev")),
        check_vma=False,
    )
```

profile of v0, /device:TPU:4, one launch (start us, length us, event | category | flops | bytes accessed | tf_op | source)
XLA Modules:
  0.0 919.5 jit_solution(7885680321525011483)
XLA Ops:
  12.5 9.9 %copy.161 = bf16[2,5,4,64,64]{1,2,0,4,3:T(4,128)(2,1)} copy(bf16[2,5,4,64,64]{4,3,2,1,0:T(8,128)(2,1)S(1)} %fusion.2) | data formatting | bytes 655360 | tf_op jit(solution)/shard_map/convert_element_type | solution.py:32
  22.3 13.3 %reshape.102 = bf16[32,2,2560]{2,1,0:T(2,128)(2,1)} reshape(bf16[4096,2,4,5]{3,2,1,0:T(4,128)(2,1)} %bitcast.255) | data formatting | bytes 655360
  35.6 16.1 %all-to-all-start = ((bf16[32,2,2560]{2,1,0:T(2,128)(2,1)}), bf16[32,2,2560]{2,1,0:T(2,128)(2,1)S(1)}, u32[]{:S(2)}, u32[]{:S(2)}) async-start(bf16[32,2,2560]{2,1,0:T(2,128)(2,1)} %reshape.102), calls=%async_computation | async-start | bytes 655360 | tf_op jit(solution)/shard_map/all_to_all | solution.py:85
  52.0 24.5 %all-to-all-done = bf16[32,2,2560]{2,1,0:T(2,128)(2,1)S(1)} async-done(((bf16[32,2,2560]{2,1,0:T(2,128)(2,1)}), bf16[32,2,2560]{2,1,0:T(2,128)(2,1)S(1)}, u32[]{:S(2)}, u32[]{:S(2)}) %all-to-all-start) | async-done | bytes 327712 | tf_op jit(solution)/shard_map/all_to_all | solution.py:85
  76.5 19.2 %reshape.103 = bf16[4096,2,4,5]{3,2,1,0:T(4,128)(2,1)} reshape(bf16[32,2,2560]{2,1,0:T(2,128)(2,1)S(1)} %all-to-all-done) | data formatting | bytes 655360
  95.7 11.4 %copy.89 = bf16[2,5,4,32,128]{4,2,3,1,0:T(4,128)(2,1)S(1)} copy(bf16[2,5,4,32,128]{1,2,0,4,3:T(4,128)(2,1)} %bitcast.256) | data formatting | bytes 655360 | tf_op jit(solution)/shard_map/all_to_all | solution.py:85
  108.7 143.3 %all-reduce.5.cloned.1.call-done = f32[5,128,128]{2,1,0:T(8,128)} async-done(((f32[5,128,128]{2,1,0:T(8,128)}), f32[5,128,128]{2,1,0:T(8,128)}) %all-reduce.5.cloned.1.call-update) | async-done | bytes 327696 | tf_op jit(solution)/shard_map/psum | solution.py:94
  252.7 6.2 gather_fusion
  258.9 5.9 scatter_custom_fusion
  265.7 151.5 %all-reduce.7.cloned.1.call-done = f32[5,128,128]{2,1,0:T(8,128)} async-done(((f32[5,128,128]{2,1,0:T(8,128)}), f32[5,128,128]{2,1,0:T(8,128)}) %all-reduce.7.cloned.1.call-update) | async-done | bytes 327696 | tf_op jit(solution)/shard_map/psum | solution.py:101
  419.6 36.8 %all_to_all.66 = bf16[2,5,128,128]{3,0,1,2:T(2,128)(2,1)S(1)} all-to-all(bf16[2,5,128,128]{3,0,1,2:T(2,128)(2,1)S(1)} %copy.95), channel_id=1, replica_groups=mesh['lev'=32,'mem'=16] {'lev'}, dimensions={2} | all-to-all | bytes 655360 | tf_op jit(solution)/shard_map/all_to_all | solution.py:112
  469.8 2.0 convolution_add_fusion.1
  473.4 11.7 %copy.163 = bf16[2,5,4,64,64]{1,2,0,4,3:T(4,128)(2,1)} copy(bf16[2,5,4,64,64]{4,3,2,1,0:T(8,128)(2,1)} %fusion.3) | data formatting | bytes 655360 | tf_op jit(solution)/shard_map/convert_element_type | solution.py:32
  485.1 13.2 %reshape.104 = bf16[32,2,2560]{2,1,0:T(2,128)(2,1)} reshape(bf16[4096,2,4,5]{3,2,1,0:T(4,128)(2,1)} %bitcast.257) | data formatting | bytes 655360
  498.3 3.9 all-to-all-start.2
  502.7 21.9 %all-to-all-done.2 = bf16[32,2,2560]{2,1,0:T(2,128)(2,1)S(1)} async-done(((bf16[32,2,2560]{2,1,0:T(2,128)(2,1)}), bf16[32,2,2560]{2,1,0:T(2,128)(2,1)S(1)}, u32[]{:S(2)}, u32[]{:S(2)}) %all-to-all-start.2) | async-done | bytes 327712 | tf_op jit(solution)/shard_map/all_to_all | solution.py:85
  524.5 19.2 %reshape.105 = bf16[4096,2,4,5]{3,2,1,0:T(4,128)(2,1)} reshape(bf16[32,2,2560]{2,1,0:T(2,128)(2,1)S(1)} %all-to-all-done.2) | data formatting | bytes 655360
  543.7 11.4 %copy.112 = bf16[2,5,4,32,128]{4,2,3,1,0:T(4,128)(2,1)S(1)} copy(bf16[2,5,4,32,128]{1,2,0,4,3:T(4,128)(2,1)} %bitcast.258) | data formatting | bytes 655360 | tf_op jit(solution)/shard_map/all_to_all | solution.py:85
  557.1 142.3 %all-reduce.9.cloned.1.call-done = f32[5,128,128]{2,1,0:T(8,128)} async-done(((f32[5,128,128]{2,1,0:T(8,128)}), f32[5,128,128]{2,1,0:T(8,128)}) %all-reduce.9.cloned.1.call-update) | async-done | bytes 327696 | tf_op jit(solution)/shard_map/psum | solution.py:94
  700.2 6.1 gather_fusion.1
  706.3 6.1 scatter_custom_fusion.1
  713.2 151.5 %all-reduce.11.cloned.1.call-done = f32[5,128,128]{2,1,0:T(8,128)} async-done(((f32[5,128,128]{2,1,0:T(8,128)}), f32[5,128,128]{2,1,0:T(8,128)}) %all-reduce.11.cloned.1.call-update) | async-done | bytes 327696 | tf_op jit(solution)/shard_map/psum | solution.py:101
  867.6 13.5 %all-to-all-start.3 = ((bf16[2,5,128,128]{3,0,1,2:T(2,128)(2,1)}), bf16[2,5,128,128]{3,0,1,2:T(2,128)(2,1)S(1)}, u32[]{:S(2)}, u32[]{:S(2)}) async-start(bf16[2,5,128,128]{3,0,1,2:T(2,128)(2,1)} %copy.120), calls=%async_computation.3 | async-start | bytes 655360 | tf_op jit(solution)/shard_map/all_to_all | solution.py:112
  882.4 22.2 %all-to-all-done.3 = bf16[2,5,128,128]{3,0,1,2:T(2,128)(2,1)S(1)} async-done(((bf16[2,5,128,128]{3,0,1,2:T(2,128)(2,1)}), bf16[2,5,128,128]{3,0,1,2:T(2,128)(2,1)S(1)}, u32[]{:S(2)}, u32[]{:S(2)}) %all-to-all-start.3) | async-done | bytes 327712 | tf_op jit(solution)/shard_map/all_to_all | solution.py:112
  (105 shorter events, 42.1 us)
Async XLA Ops:
  7.2 100.0 %copy-start = (bf16[5,128,128]{2,1,0:T(8,128)(2,1)S(1)}, bf16[5,128,128]{2,1,0:T(8,128)(2,1)}, u32[]{:S(2)}) copy-start(bf16[5,128,128]{2,1,0:T(8,128)(2,1)} %param.16) | copy-start | bytes 491524
  8.0 2.8 copy-start.7
  22.3 29.4 %copy-start.9 = (bf16[2,5,128,128]{3,2,1,0:T(8,128)(2,1)S(1)}, bf16[2,5,128,128]{3,2,1,0:T(8,128)(2,1)}, u32[]{:S(2)}) copy-start(bf16[2,5,128,128]{3,2,1,0:T(8,128)(2,1)} %param.13) | copy-start | bytes 983044
  35.6 40.9 %all-to-all-start = ((bf16[32,2,2560]{2,1,0:T(2,128)(2,1)}), bf16[32,2,2560]{2,1,0:T(2,128)(2,1)S(1)}, u32[]{:S(2)}, u32[]{:S(2)}) async-start(bf16[32,2,2560]{2,1,0:T(2,128)(2,1)} %reshape.102), calls=%async_computation | async-start | bytes 655360 | tf_op jit(solution)/shard_map/all_to_all | solution.py:85
  51.7 200.2 %all-reduce.5.cloned.1.call-start = ((), (), s32[]{:S(2)}) async-start(), calls=%async_computation.4 | async-start | bytes 655360 | tf_op jit(solution)/shard_map/psum | solution.py:94
  107.1 1.3 copy-start.13
  107.1 1.4 copy-start.1
  107.1 1.4 copy-start.8
  108.4 308.8 %all-reduce.7.cloned.1.call-start = ((), (), s32[]{:S(2)}) async-start(), calls=%async_computation.5 | async-start | bytes 655360 | tf_op jit(solution)/shard_map/psum | solution.py:101
  108.5 150.5 %copy-start.14 = (s32[1024]{0:T(1024)}, s32[1024]{0:T(1024)S(1)}, u32[]{:S(2)}) copy-start(s32[1024]{0:T(1024)S(1)} %get-tuple-element.11) | copy-start | bytes 12292
  252.7 6.2 copy-start.10
  252.7 6.2 copy-start.11
  252.7 6.2 copy-start.12
  264.9 0.7 copy-start.6
  465.6 1.0 copy-start.4
  498.3 26.2 %all-to-all-start.2 = ((bf16[32,2,2560]{2,1,0:T(2,128)(2,1)}), bf16[32,2,2560]{2,1,0:T(2,128)(2,1)S(1)}, u32[]{:S(2)}, u32[]{:S(2)}) async-start(bf16[32,2,2560]{2,1,0:T(2,128)(2,1)} %reshape.104), calls=%async_computation.2 | async-start | bytes 655360 | tf_op jit(solution)/shard_map/all_to_all | solution.py:85
  502.2 197.2 %all-reduce.9.cloned.1.call-start = ((), (), s32[]{:S(2)}) async-start(), calls=%async_computation.6 | async-start | bytes 655360 | tf_op jit(solution)/shard_map/psum | solution.py:94
  555.1 1.3 copy-start.2
  556.4 308.4 %all-reduce.11.cloned.1.call-start = ((), (), s32[]{:S(2)}) async-start(), calls=%async_computation.7 | async-start | bytes 655360 | tf_op jit(solution)/shard_map/psum | solution.py:101
  712.5 0.7 copy-start.5
  865.9 15.2 %copy-start.3 = (f32[5,128,128]{2,1,0:T(8,128)S(1)}, f32[5,128,128]{2,1,0:T(8,128)}, u32[]{:S(2)}) copy-start(f32[5,128,128]{2,1,0:T(8,128)} %all-reduce.11.cloned.1.call-done) | copy-start | bytes 983044
  867.6 37.0 %all-to-all-start.3 = ((bf16[2,5,128,128]{3,0,1,2:T(2,128)(2,1)}), bf16[2,5,128,128]{3,0,1,2:T(2,128)(2,1)S(1)}, u32[]{:S(2)}, u32[]{:S(2)}) async-start(bf16[2,5,128,128]{3,0,1,2:T(2,128)(2,1)} %copy.120), calls=%async_computation.3 | async-start | bytes 655360 | tf_op jit(solution)/shard_map/all_to_all | solution.py:112
Sparse Core Ops, SparseCore 0:
  108.5 143.3 all-reduce.4
  265.8 151.3 all-reduce.6
  556.5 142.9 all-reduce.8
  713.3 151.3 all-reduce.10
where the time goes:
time: 922 us; the launch traced here: 920 us
  waiting for transfers between devices  657 us (71%)
  local copies, waits for them, and re-layouts  135 us (15%)
  blocking collectives  36.8 us (4%)
  starting transfers between devices  33.9 us (4%)
  matrix products  24.7 us (3%)
  other arithmetic  17.5 us (2%)
  between operations  14.4 us (2%)
    psum x2, waiting for transfers between devices, on_device(): gradient_field_total = lax.psum(placed, 'mem')  303 us
    psum x2, waiting for transfers between devices, on_device(): ens = lax.psum(partial_value, 'mem')  286 us
    unnamed x37, local copies, waits for them, and re-layouts  67.9 us
    all_to_all x2, waiting for transfers between devices, on_device(): lax.all_to_all(local, 'lev', split_axis=3, concat_axis=2, tiled=True)  46.4 us
    all_to_all x1, blocking collectives, on_device(): lax.all_to_all(backward_field, 'lev', split_axis=2, concat_axis=3, tiled=...  36.8 us
    all_to_all x2, local copies, waits for them, and re-layouts, on_device(): lax.all_to_all(local, 'lev', split_axis=3, concat_axis=2, tiled=True)  22.9 us
    all_to_all x1, waiting for transfers between devices, on_device(): lax.all_to_all(backward_field, 'lev', split_axis=2, concat_axis=3, tiled=...  22.2 us
    convert_element_type x2, local copies, waits for them, and re-layouts, horizontal(): return total.reshape(field.shape).astype(jnp.bfloat16)  21.5 us
  transfers between devices with their start and end apart: 7, of which 7 were waited for; matrix products, arithmetic and copies ran while one was open for 0% of the time, Pallas kernels for 0%

commit v1 on v0

--- a/solution.py
+++ b/solution.py
@@ -82,7 +82,19 @@
     static_forward = static_vertical_root.astype(jnp.float32)
     for turn in range(ITERS):
         local = horizontal(control, tiles, picks)
-        columns = lax.all_to_all(local, "lev", split_axis=3, concat_axis=2, tiled=True)
+
+        def perform_rails(obj, peer_axis, which_dim, where_dim):
+            return jnp.concatenate(
+                lax.all_to_all(
+                    jnp.stack(jnp.split(obj, lax.axis_size(peer_axis), which_dim), 0),
+                    peer_axis,
+                    0,
+                    0,
+                ),
+                where_dim,
+            )
+
+        columns = perform_rails(local, "lev", 3, 2)
         vertical = jnp.einsum("vlk,mvkc->mvlc", vert, columns, preferred_element_type=jnp.float32)
         partial_value = jnp.sum(vertical * perturb.astype(jnp.float32), axis=0)
         static_portion = jnp.einsum(

time: 922 us -> 852 us (0.924)
  local copies, waits for them, and re-layouts: 135 us -> 66.8 us
    unnamed x37 -> x95, local copies, waits for them, and re-layouts: 67.9 us -> 40.7 us
    all_to_all x2 -> x0, local copies, waits for them, and re-layouts: 22.9 us -> none  [on_device(): lax.all_to_all(local, 'lev', split_axis=3, concat_axis=2, tiled=True)]
    convert_element_type x2, local copies, waits for them, and re-layouts: 21.5 us -> 2 us  [horizontal(): return total.reshape(field.shape).astype(jnp.bfloat16)]
where the time goes in v1:
time: 852 us; the launch traced here: 851 us
  waiting for transfers between devices  657 us (77%)
  local copies, waits for them, and re-layouts  66.8 us (8%)
  blocking collectives  36.8 us (4%)
  starting transfers between devices  33.9 us (4%)
  matrix products  24.7 us (3%)
  other arithmetic  17.5 us (2%)
  between operations  14.4 us (2%)
    psum x2, waiting for transfers between devices, on_device(): gradient_field_total = lax.psum(placed, 'mem')  303 us
    psum x2, waiting for transfers between devices, on_device(): ens = lax.psum(partial_value, 'mem')  285 us
    all_to_all x2, waiting for transfers between devices, perform_rails(): lax.all_to_all(jnp.stack(jnp.split(obj, lax.axis_size(peer_axis), which_d...  46.6 us
    unnamed x95, local copies, waits for them, and re-layouts  40.7 us
    all_to_all x1, blocking collectives, on_device(): lax.all_to_all(backward_field, 'lev', split_axis=2, concat_axis=3, tiled=...  36.8 us
    all_to_all x1, waiting for transfers between devices, on_device(): lax.all_to_all(backward_field, 'lev', split_axis=2, concat_axis=3, tiled=...  22.2 us
    all_to_all x2, starting transfers between devices, perform_rails(): lax.all_to_all(jnp.stack(jnp.split(obj, lax.axis_size(peer_axis), which_d...  20 us
  transfers between devices with their start and end apart: 7, of which 7 were waited for; matrix products, arithmetic and copies ran while one was open for 0% of the time, Pallas kernels for 0%

profile of v1, /device:TPU:4, one launch (start us, length us, event | category | flops | bytes accessed | tf_op | source)
XLA Modules:
  0.0 851.3 jit_solution(6151782144119729264)
XLA Ops:
  8.0 1.6 reshape.55
  9.6 1.2 fusion.5
  32.4 16.1 %all-to-all-start = ((bf16[32,2,5,4,128]{4,3,2,1,0:T(4,128)(2,1)}), bf16[32,2,5,4,128]{4,3,2,1,0:T(4,128)(2,1)S(1)}, u32[]{:S(2)}, u32[]{:S(2)}) async-start(bf16[32,2,5,4,128]{4,3,2,1,0:T(4,128)(2,1)} %constant_dynamic-update-slice_fusion), calls=%async_computation | async-start | bytes 655360 | tf_op jit(solution)/shard_map/all_to_all | solution.py:88
  48.7 24.5 %all-to-all-done = bf16[32,2,5,4,128]{4,3,2,1,0:T(4,128)(2,1)S(1)} async-done(((bf16[32,2,5,4,128]{4,3,2,1,0:T(4,128)(2,1)}), bf16[32,2,5,4,128]{4,3,2,1,0:T(4,128)(2,1)S(1)}, u32[]{:S(2)}, u32[]{:S(2)}) %all-to-all-start) | async-done | bytes 327712 | tf_op jit(solution)/shard_map/all_to_all | solution.py:88
  75.0 143.2 %all-reduce.5.cloned.1.call-done = f32[5,128,128]{2,1,0:T(8,128)} async-done(((f32[5,128,128]{2,1,0:T(8,128)}), f32[5,128,128]{2,1,0:T(8,128)}) %all-reduce.5.cloned.1.call-update) | async-done | bytes 327696 | tf_op jit(solution)/shard_map/psum | solution.py:106
  218.9 6.2 gather_fusion
  225.1 5.9 scatter_custom_fusion
  231.9 151.5 %all-reduce.7.cloned.1.call-done = f32[5,128,128]{2,1,0:T(8,128)} async-done(((f32[5,128,128]{2,1,0:T(8,128)}), f32[5,128,128]{2,1,0:T(8,128)}) %all-reduce.7.cloned.1.call-update) | async-done | bytes 327696 | tf_op jit(solution)/shard_map/psum | solution.py:113
  385.8 36.8 %all_to_all.40 = bf16[2,5,128,128]{3,0,1,2:T(2,128)(2,1)S(1)} all-to-all(bf16[2,5,128,128]{3,0,1,2:T(2,128)(2,1)S(1)} %copy.113), channel_id=1, replica_groups=mesh['lev'=32,'mem'=16] {'lev'}, dimensions={2} | all-to-all | bytes 655360 | tf_op jit(solution)/shard_map/all_to_all | solution.py:124
  428.3 1.8 fusion.1
  430.1 1.7 copy.120
  434.3 1.8 convolution_add_fusion.2
  436.1 2.0 convolution_add_fusion.1
  438.1 1.5 fusion.3
  439.6 1.5 convert_element_type.140
  460.6 3.9 all-to-all-start.2
  464.7 22.1 %all-to-all-done.2 = bf16[32,2,5,4,128]{4,3,2,1,0:T(4,128)(2,1)S(1)} async-done(((bf16[32,2,5,4,128]{4,3,2,1,0:T(4,128)(2,1)}), bf16[32,2,5,4,128]{4,3,2,1,0:T(4,128)(2,1)S(1)}, u32[]{:S(2)}, u32[]{:S(2)}) %all-to-all-start.2) | async-done | bytes 327712 | tf_op jit(solution)/shard_map/all_to_all | solution.py:88
  489.1 142.1 %all-reduce.9.cloned.1.call-done = f32[5,128,128]{2,1,0:T(8,128)} async-done(((f32[5,128,128]{2,1,0:T(8,128)}), f32[5,128,128]{2,1,0:T(8,128)}) %all-reduce.9.cloned.1.call-update) | async-done | bytes 327696 | tf_op jit(solution)/shard_map/psum | solution.py:106
  632.0 6.1 gather_fusion.1
  638.1 6.1 scatter_custom_fusion.1
  645.0 151.5 %all-reduce.11.cloned.1.call-done = f32[5,128,128]{2,1,0:T(8,128)} async-done(((f32[5,128,128]{2,1,0:T(8,128)}), f32[5,128,128]{2,1,0:T(8,128)}) %all-reduce.11.cloned.1.call-update) | async-done | bytes 327696 | tf_op jit(solution)/shard_map/psum | solution.py:113
  798.2 1.3 copy.137
  799.4 13.5 %all-to-all-start.3 = ((bf16[2,5,128,128]{3,0,1,2:T(2,128)(2,1)}), bf16[2,5,128,128]{3,0,1,2:T(2,128)(2,1)S(1)}, u32[]{:S(2)}, u32[]{:S(2)}) async-start(bf16[2,5,128,128]{3,0,1,2:T(2,128)(2,1)} %copy.137), calls=%async_computation.3 | async-start | bytes 655360 | tf_op jit(solution)/shard_map/all_to_all | solution.py:124
  814.2 22.2 %all-to-all-done.3 = bf16[2,5,128,128]{3,0,1,2:T(2,128)(2,1)S(1)} async-done(((bf16[2,5,128,128]{3,0,1,2:T(2,128)(2,1)}), bf16[2,5,128,128]{3,0,1,2:T(2,128)(2,1)S(1)}, u32[]{:S(2)}, u32[]{:S(2)}) %all-to-all-start.3) | async-done | bytes 327712 | tf_op jit(solution)/shard_map/all_to_all | solution.py:124
  (165 shorter events, 70.6 us)
Async XLA Ops:
  7.2 66.3 %copy-start = (bf16[5,128,128]{2,1,0:T(8,128)(2,1)S(1)}, bf16[5,128,128]{2,1,0:T(8,128)(2,1)}, u32[]{:S(2)}) copy-start(bf16[5,128,128]{2,1,0:T(8,128)(2,1)} %param.16) | copy-start | bytes 491524
  8.0 2.8 copy-start.7
  12.5 36.1 %copy-start.9 = (bf16[2,5,128,128]{3,2,1,0:T(8,128)(2,1)S(1)}, bf16[2,5,128,128]{3,2,1,0:T(8,128)(2,1)}, u32[]{:S(2)}) copy-start(bf16[2,5,128,128]{3,2,1,0:T(8,128)(2,1)} %param.13) | copy-start | bytes 983044
  32.4 40.9 %all-to-all-start = ((bf16[32,2,5,4,128]{4,3,2,1,0:T(4,128)(2,1)}), bf16[32,2,5,4,128]{4,3,2,1,0:T(4,128)(2,1)S(1)}, u32[]{:S(2)}, u32[]{:S(2)}) async-start(bf16[32,2,5,4,128]{4,3,2,1,0:T(4,128)(2,1)} %constant_dynamic-update-slice_fusion), calls=%async_computation | async-start | bytes 655360 | tf_op jit(solution)/shard_map/all_to_all | solution.py:88
  48.5 169.7 %all-reduce.5.cloned.1.call-start = ((), (), s32[]{:S(2)}) async-start(), calls=%async_computation.4 | async-start | bytes 655360 | tf_op jit(solution)/shard_map/psum | solution.py:106
  73.3 1.4 copy-start.13
  73.3 1.5 copy-start.1
  73.3 1.5 copy-start.8
  74.7 308.7 %all-reduce.7.cloned.1.call-start = ((), (), s32[]{:S(2)}) async-start(), calls=%async_computation.5 | async-start | bytes 655360 | tf_op jit(solution)/shard_map/psum | solution.py:113
  74.7 150.4 %copy-start.14 = (s32[1024]{0:T(1024)}, s32[1024]{0:T(1024)S(1)}, u32[]{:S(2)}) copy-start(s32[1024]{0:T(1024)S(1)} %get-tuple-element.9) | copy-start | bytes 12292
  218.9 6.2 copy-start.10
  218.9 6.2 copy-start.11
  218.9 6.2 copy-start.12
  231.1 0.7 copy-start.6
  431.8 1.0 copy-start.4
  460.6 26.2 %all-to-all-start.2 = ((bf16[32,2,5,4,128]{4,3,2,1,0:T(4,128)(2,1)}), bf16[32,2,5,4,128]{4,3,2,1,0:T(4,128)(2,1)S(1)}, u32[]{:S(2)}, u32[]{:S(2)}) async-start(bf16[32,2,5,4,128]{4,3,2,1,0:T(4,128)(2,1)} %constant_dynamic-update-slice_fusion.32), calls=%async_computation.2 | async-start | bytes 655360 | tf_op jit(solution)/shard_map/all_to_all | solution.py:88
  464.5 166.8 %all-reduce.9.cloned.1.call-start = ((), (), s32[]{:S(2)}) async-start(), calls=%async_computation.6 | async-start | bytes 655360 | tf_op jit(solution)/shard_map/psum | solution.py:106
  486.8 1.6 copy-start.2
  488.2 308.4 %all-reduce.11.cloned.1.call-start = ((), (), s32[]{:S(2)}) async-start(), calls=%async_computation.7 | async-start | bytes 655360 | tf_op jit(solution)/shard_map/psum | solution.py:113
  644.3 0.7 copy-start.5
  797.7 15.2 %copy-start.3 = (f32[5,128,128]{2,1,0:T(8,128)S(1)}, f32[5,128,128]{2,1,0:T(8,128)}, u32[]{:S(2)}) copy-start(f32[5,128,128]{2,1,0:T(8,128)} %all-reduce.11.cloned.1.call-done) | copy-start | bytes 983044
  799.4 37.0 %all-to-all-start.3 = ((bf16[2,5,128,128]{3,0,1,2:T(2,128)(2,1)}), bf16[2,5,128,128]{3,0,1,2:T(2,128)(2,1)S(1)}, u32[]{:S(2)}, u32[]{:S(2)}) async-start(bf16[2,5,128,128]{3,0,1,2:T(2,128)(2,1)} %copy.137), calls=%async_computation.3 | async-start | bytes 655360 | tf_op jit(solution)/shard_map/all_to_all | solution.py:124
Sparse Core Ops, SparseCore 0:
  74.8 143.3 all-reduce.4
  232.0 151.3 all-reduce.6
  488.3 142.9 all-reduce.8
  645.1 151.3 all-reduce.10
